TPU v7x, 512 devices: a whole 4x4x16 slice. The times are simulated.
512 devices in a mesh: ctx: 32 (over z, core), tp: 16 (over x, y).
Axes of the slice: x: 4, y: 4, z: 16, core: 2. Of those that a mesh axis runs over, the one named last changes fastest.
Arguments:
- queries: bfloat16 [8192, 8192], P('ctx', 'tp'), may hold values from -6 to 6
- keys: bfloat16 [8192, 8192], P('ctx', 'tp'), may hold values from -0.0625 to 0.0625
- values: bfloat16 [8192, 8192], P('ctx', 'tp'), may hold values from -6 to 6
- log_keep: float32 [64, 8192], P('tp', 'ctx'), may hold values from -1 to 0, as said below
- state_in: float32 [64, 128, 128], P('tp'), may hold values from -6 to 6
- norm_gain: float32 [8192], P('tp'), may hold values from 0.1 to 1.9
- out_weight: bfloat16 [8192, 6144], P('tp', 'ctx'), may hold values from -0.125 to 0.125
Outputs:
- normed: bfloat16 [8192, 8192], P('ctx', 'tp')
- state_out: float32 [64, 128, 128], P('tp', 'ctx')
- layer_out: bfloat16 [8192, 6144], P('ctx', 'tp')
Inputs may be any that keep to these rules, and one draw needn't show every extreme that they name: `log_keep`: every entry is a logarithm of a keep factor, so at most 0.
All inputs are finite; a program needn't handle non-finite values.
Results may differ from a plain program's by a relative error of at most 0.014.
Values may be sent and summed in bfloat16 or wider, within the bound.
No kernel may reach another device: no remote copies, remote signals or barrier semaphores. Data moves between devices by JAX's collectives and lax.ppermute only.
A program may use at most 64 MiB of HBM per device.

v0:
```python
import jax
import jax.numpy as jnp
from jax import lax
from jax.sharding import Mesh, PartitionSpec as P

H = 64
DH = 128
EPSILON = 1e-06
CTX = ("za", "zb", "core")
INNER = ("zb", "core")
TP = ("x", "y")
HIGH = lax.Precision.HIGHEST
BF16 = jnp.bfloat16
F32 = jnp.float32


def split3(x):
    hi = lax.reduce_precision(x, 8, 7)
    rest = x - hi
    mid = lax.reduce_precision(rest, 8, 7)
    low = rest - mid
    return jnp.stack([hi.astype(BF16), mid.astype(BF16), low.astype(BF16)])


def join3(parts):
    parts = parts.astype(F32)
    return parts[0] + (parts[1] + parts[2])


def with_rows(block, vector):
    width = block.shape[-1]
    flat = split3(vector).reshape(-1)
    tail = jnp.pad(flat, (0, 16 * width - flat.shape[0])).reshape(16, width)
    lead = block.shape[:-2]
    tail = jnp.broadcast_to(tail, lead + tail.shape)
    return jnp.concatenate([block, tail], axis=-2)


def rows_of(tail, n):
    count = tail.shape[0]
    flat = tail.reshape(count, -1)[:, : 3 * n].reshape(count, 3, n)
    return jnp.sum(join3(jnp.moveaxis(flat, 1, 0)), axis=0)


def mixer(logs):
    count, heads = logs.shape
    upto = jnp.concatenate([jnp.zeros((1, heads), F32), jnp.cumsum(logs, axis=0)])
    before = jnp.arange(count)[None, :] < jnp.arange(count + 1)[:, None]
    gap = upto[:, None] - upto[None, 1:]
    factor = jnp.where(before[:, :, None], jnp.exp(jnp.minimum(gap, 0.0)), 0.0)
    return (upto, factor)


def per_device(queries, keys, values, log_keep, state_in, norm_gain, out_weight):
    tokens = queries.shape[0]
    heads = log_keep.shape[0]
    parts = lax.axis_size(CTX)
    quads, inner = (lax.axis_size("za"), lax.axis_size(INNER))
    rows = DH // parts
    slab = heads * quads * rows
    nx, ny = (lax.axis_size("x"), lax.axis_size("y"))
    swap = [(a * ny + b, b * ny + a) for a in range(ny) for b in range(ny)]
    moved = lax.ppermute(out_weight.T, ("zb", "y"), swap)
    gathered = lax.all_gather(moved, CTX, axis=0, tiled=True)
    cols = out_weight.shape[1] * parts // (nx * ny)
    gathered = gathered.reshape(nx, ny, cols, out_weight.shape[0])
    q = queries.reshape(tokens, heads, DH)
    k = keys.reshape(tokens, heads, DH)
    v = values.reshape(tokens, heads, DH)
    within = jnp.cumsum(log_keep, axis=1)
    own_log = within[:, -1]
    key_factor = jnp.exp(own_log[:, None] - within).T
    kdec = (k * key_factor[:, :, None]).astype(BF16)
    inc = jnp.einsum("shd,she->hde", kdec, v, preferred_element_type=F32)
    out = inc.astype(BF16).reshape(heads, quads, inner, rows, DH)
    out = out.transpose(2, 0, 1, 3, 4).reshape(inner, slab, DH)
    logs = jnp.pad(split3(own_log), ((0, 5), (0, DH - heads)))
    logs = jnp.broadcast_to(logs[None], (inner,) + logs.shape)
    got = lax.all_to_all(jnp.concatenate([out, logs], axis=1), INNER, 0, 0, tiled=True)
    causal = jnp.tril(jnp.ones((tokens, tokens), dtype=bool))
    spread = within[:, :, None] - within[:, None, :]
    decay = jnp.where(causal, jnp.exp(jnp.minimum(spread, 0.0)), 0.0)
    scores = jnp.einsum("shd,thd->hst", q, k, preferred_element_type=F32)
    weights = (scores * decay).astype(BF16)
    intra = jnp.einsum("hst,thd->shd", weights, v, preferred_element_type=F32)
    incs = got[:, :slab].astype(F32).reshape(inner, heads, -1)
    upto, mixing = mixer(join3(jnp.moveaxis(got[:, slab : slab + 3, :heads], 1, 0)))
    local = jnp.einsum("cjh,jhn->chn", mixing, incs, precision=HIGH)
    total_log = jnp.pad(upto[inner], (0, DH - heads))
    total_log = jnp.pad(total_log[None], ((0, 7), (0, 0)))
    total = jnp.concatenate([local[inner].reshape(slab, DH), total_log])
    totals = lax.all_to_all(
        jnp.broadcast_to(total[None], (quads,) + total.shape), "za", 0, 0, tiled=True
    )
    after, across = mixer(totals[:, slab, :heads])
    first = lax.dynamic_index_in_dim(
        state_in.reshape(heads, quads, inner, rows, DH), lax.axis_index(INNER), 2, keepdims=False
    ).reshape(heads, -1)
    bounds = jnp.einsum(
        "cjh,jhn->chn", across, totals[:, :slab].reshape(quads, heads, -1), precision=HIGH
    )
    bounds = bounds + jnp.exp(after)[:, :, None] * first[None]
    quad = lax.axis_index("za")
    final = lax.dynamic_index_in_dim(
        bounds[quads].reshape(heads, quads, rows, DH), quad, 1, keepdims=False
    )
    opening = lax.dynamic_index_in_dim(bounds, quad, 0, keepdims=False)
    states = local[:inner] + jnp.exp(upto[:inner])[:, :, None] * opening[None]
    states = states.astype(BF16).reshape(inner, slab, DH)
    back = lax.all_to_all(states, INNER, 0, 0, tiled=True)
    start = back.reshape(inner, heads, quads, rows, DH).transpose(1, 2, 0, 3, 4)
    start = start.reshape(heads, DH, DH)
    inter = jnp.einsum("shd,hde->she", q, start, preferred_element_type=F32)
    inter = inter * jnp.exp(within).T[:, :, None]
    attended = (intra + inter).reshape(tokens, heads * DH)
    squares = jnp.sum(attended * attended, axis=1)
    gained = attended * norm_gain
    message = with_rows(gained.astype(BF16), squares)
    message = jnp.broadcast_to(message[None], (ny,) + message.shape)
    acts = lax.all_to_all(message, "y", 0, 0, tiled=True)
    squares = rows_of(acts[:, tokens:], tokens)
    partial = jnp.stack(
        [
            sum(
                (
                    lax.dot_general(
                        acts[i, :tokens],
                        gathered[j, i],
                        (((1,), (1,)), ((), ())),
                        preferred_element_type=F32,
                    )
                    for i in range(ny)
                )
            ).astype(BF16)
            for j in range(nx)
        ]
    )
    shares = lax.all_to_all(with_rows(partial, squares), "x", 0, 0, tiled=True)
    squares = rows_of(shares[:, tokens:], tokens)
    scale = lax.rsqrt(squares / (H * DH) + EPSILON)[:, None]
    normed = (attended * scale * norm_gain).astype(BF16)
    layer_out = (jnp.sum(shares[:, :tokens].astype(F32), axis=0) * scale).astype(BF16)
    return (normed, final, layer_out)


def solution(mesh):
    fine = Mesh(mesh.devices.reshape(4, 4, 2, 4, 4), CTX + TP)
    return jax.shard_map(
        per_device,
        mesh=fine,
        in_specs=(
            P(CTX, TP),
            P(CTX, TP),
            P(CTX, TP),
            P(TP, CTX),
            P(TP, None, None),
            P(TP),
            P(TP, CTX),
        ),
        out_specs=(P(CTX, TP), P(TP, CTX, None), P(CTX, TP)),
        check_vma=False,
    )
```

profile of v0, /device:TPU:1, one launch (start us, length us, event | category | flops | bytes accessed | tf_op | source)
XLA Modules:
  0.0 151.2 jit_solution(5033377000865142325)
XLA Ops:
  7.2 1.7 %collective-permute-start = (bf16[192,512]{1,0:T(8,128)(2,1)}, bf16[192,512]{1,0:T(8,128)(2,1)S(1)}, u32[]{:S(2)}, u32[]{:S(2)}) collective-permute-start(bf16[192,512]{1,0:T(8,128)(2,1)} %bitcast.227), channel_id=1, source_target_pairs={{0,0},{1,32},{2,64},{3,96},{32,1},{33,33},{34,65},{35,97},{64,2},{... | collective-permute-start | bytes 589832 | tf_op jit(solution)/shard_map/ppermute | solution.py:63
  8.9 0.7 copy-done.2
  9.6 0.7 reshape.265
  10.3 1.2 reduce-window.6
  12.1 1.1 copy.88
  13.3 1.2 convolution_convert_fusion
  14.6 0.7 pad_maximum_fusion.2
  15.2 20.1 %all-to-all-start = ((bf16[8,72,128]{2,1,0:T(8,128)(2,1)}), bf16[8,72,128]{2,1,0:T(8,128)(2,1)S(1)}, u32[]{:S(2)}, u32[]{:S(2)}) async-start(bf16[8,72,128]{2,1,0:T(8,128)(2,1)} %pad_maximum_fusion.2), calls=%async_computation | async-start | bytes 294912 | tf_op jit(solution)/shard_map/all_to_all | solution.py:79
  35.3 6.0 %all-to-all-done = bf16[8,72,128]{2,1,0:T(8,128)(2,1)S(1)} async-done(((bf16[8,72,128]{2,1,0:T(8,128)(2,1)}), bf16[8,72,128]{2,1,0:T(8,128)(2,1)S(1)}, u32[]{:S(2)}, u32[]{:S(2)}) %all-to-all-start) | async-done | bytes 147488 | tf_op jit(solution)/shard_map/all_to_all | solution.py:79
  42.5 0.7 broadcast_in_dim.38
  43.1 13.7 %all-to-all-start.1 = ((f32[4,72,128]{2,1,0:T(8,128)}), f32[4,72,128]{2,1,0:T(8,128)S(1)}, u32[]{:S(2)}, u32[]{:S(2)}) async-start(f32[4,72,128]{2,1,0:T(8,128)} %broadcast_in_dim.38), calls=%async_computation.1 | async-start | bytes 294912 | tf_op jit(solution)/shard_map/all_to_all | solution.py:92
  56.9 0.8 constant_dynamic-slice_fusion.1
  57.7 17.3 %all-to-all-done.1 = f32[4,72,128]{2,1,0:T(8,128)S(1)} async-done(((f32[4,72,128]{2,1,0:T(8,128)}), f32[4,72,128]{2,1,0:T(8,128)S(1)}, u32[]{:S(2)}, u32[]{:S(2)}) %all-to-all-start.1) | async-done | bytes 147488 | tf_op jit(solution)/shard_map/all_to_all | solution.py:92
  75.4 0.5 fusion
  76.2 0.7 reshape.273
  77.0 4.3 %all-to-all-start.2 = ((bf16[8,64,128]{2,1,0:T(8,128)(2,1)}), bf16[8,64,128]{2,1,0:T(8,128)(2,1)S(1)}, u32[]{:S(2)}, u32[]{:S(2)}) async-start(bf16[8,64,128]{2,1,0:T(8,128)(2,1)} %reshape.273), calls=%async_computation.2 | async-start | bytes 262144 | tf_op jit(solution)/shard_map/all_to_all | solution.py:110
  81.3 0.6 convolution_bitcast_fusion.3
  81.9 5.7 %all-to-all-done.2 = bf16[8,64,128]{2,1,0:T(8,128)(2,1)S(1)} async-done(((bf16[8,64,128]{2,1,0:T(8,128)(2,1)}), bf16[8,64,128]{2,1,0:T(8,128)(2,1)S(1)}, u32[]{:S(2)}, u32[]{:S(2)}) %all-to-all-start.2) | async-done | bytes 131104 | tf_op jit(solution)/shard_map/all_to_all | solution.py:110
  88.6 20.5 %all_to_all.25 = bf16[4,272,512]{2,1,0:T(8,128)(2,1)S(1)} all-to-all(bf16[4,272,512]{2,1,0:T(8,128)(2,1)S(1)} %broadcast_in_dim.40), channel_id=1, replica_groups=mesh['za'=4,'zb'=4,'core'=2,'x'=4,'y'=4] {'y'}, dimensions={0} | all-to-all | bytes 2228224 | tf_op jit(solution)/shard_map/all_to_all | solution.py:120
  109.2 4.1 %all-gather.2.cloned.1.call-done = bf16[6144,512]{1,0:T(8,128)(2,1)} async-done(((bf16[192,512]{1,0:T(8,128)(2,1)}), bf16[6144,512]{1,0:T(8,128)(2,1)}) %all-gather.2.cloned.1.call-update) | async-done | bytes 6291472 | tf_op jit(solution)/shard_map/all_gather | solution.py:64
  113.4 1.5 fusion.23
  114.8 1.7 %fusion.22 = f32[256,384]{1,0:T(8,128)S(1)} fusion(bf16[4,4,384,512]{3,2,1,0:T(8,128)(2,1)} %bitcast.189, bf16[4,272,512]{2,1,0:T(8,128)(2,1)S(1)} %all_to_all.25), kind=kOutput, calls=%fused_computation.57 | convolution fusion | flops 100663296 | bytes 1048576 | tf_op jit(solution)/shard_map/dot_general | solution.py:126
  116.5 1.3 fusion.21
  117.8 1.3 fusion.20
  119.1 1.3 convolution_add_fusion.11
  120.5 1.3 convolution_add_fusion.10
  125.1 1.0 pad_maximum_fusion
  126.1 4.1 %all-to-all-start.4 = ((bf16[4,272,384]{2,1,0:T(8,128)(2,1)}), bf16[4,272,384]{2,1,0:T(8,128)(2,1)S(1)}, u32[]{:S(2)}, u32[]{:S(2)}) async-start(bf16[4,272,384]{2,1,0:T(8,128)(2,1)} %pad_maximum_fusion), calls=%async_computation.4 | async-start | bytes 1671168 | tf_op jit(solution)/shard_map/all_to_all | solution.py:138
  130.2 0.6 dynamic-slice_bitcast_fusion
  130.8 11.7 %all-to-all-done.4 = bf16[4,272,384]{2,1,0:T(8,128)(2,1)S(1)} async-done(((bf16[4,272,384]{2,1,0:T(8,128)(2,1)}), bf16[4,272,384]{2,1,0:T(8,128)(2,1)S(1)}, u32[]{:S(2)}, u32[]{:S(2)}) %all-to-all-start.4) | async-done | bytes 835616 | tf_op jit(solution)/shard_map/all_to_all | solution.py:138
  142.6 0.8 multiply_convert_fusion
  143.5 0.8 multiply_convert_fusion.3
  (95 shorter events, 7.1 us)
Async XLA Ops:
  7.2 74.1 %copy-start = (bf16[256,512]{1,0:T(8,128)(2,1)S(1)}, bf16[256,512]{1,0:T(8,128)(2,1)}, u32[]{:S(2)}) copy-start(bf16[256,512]{1,0:T(8,128)(2,1)} %param.7) | copy-start | bytes 786436
  7.2 106.2 %all-gather.2.cloned.1.call-start = ((), (), s32[]{:S(2)}) async-start(), calls=%async_computation.5 | async-start | bytes 6488064 | tf_op jit(solution)/shard_map/all_gather | solution.py:64
  7.2 1.7 %collective-permute-start = (bf16[192,512]{1,0:T(8,128)(2,1)}, bf16[192,512]{1,0:T(8,128)(2,1)S(1)}, u32[]{:S(2)}, u32[]{:S(2)}) collective-permute-start(bf16[192,512]{1,0:T(8,128)(2,1)} %bitcast.227), channel_id=1, source_target_pairs={{0,0},{1,32},{2,64},{3,96},{32,1},{33,33},{34,65},{35,97},{64,2},{... | collective-permute-start | bytes 589832 | tf_op jit(solution)/shard_map/ppermute | solution.py:63
  8.9 0.7 copy-start.2
  15.2 26.1 %all-to-all-start = ((bf16[8,72,128]{2,1,0:T(8,128)(2,1)}), bf16[8,72,128]{2,1,0:T(8,128)(2,1)S(1)}, u32[]{:S(2)}, u32[]{:S(2)}) async-start(bf16[8,72,128]{2,1,0:T(8,128)(2,1)} %pad_maximum_fusion.2), calls=%async_computation | async-start | bytes 294912 | tf_op jit(solution)/shard_map/all_to_all | solution.py:79
  42.2 39.1 %copy-start.4 = (bf16[256,512]{1,0:T(8,128)(2,1)S(1)}, bf16[256,512]{1,0:T(8,128)(2,1)}, u32[]{:S(2)}) copy-start(bf16[256,512]{1,0:T(8,128)(2,1)} %param.9) | copy-start | bytes 786436
  43.1 31.9 %all-to-all-start.1 = ((f32[4,72,128]{2,1,0:T(8,128)}), f32[4,72,128]{2,1,0:T(8,128)S(1)}, u32[]{:S(2)}, u32[]{:S(2)}) async-start(f32[4,72,128]{2,1,0:T(8,128)} %broadcast_in_dim.38), calls=%async_computation.1 | async-start | bytes 294912 | tf_op jit(solution)/shard_map/all_to_all | solution.py:92
  77.0 10.6 %all-to-all-start.2 = ((bf16[8,64,128]{2,1,0:T(8,128)(2,1)}), bf16[8,64,128]{2,1,0:T(8,128)(2,1)S(1)}, u32[]{:S(2)}, u32[]{:S(2)}) async-start(bf16[8,64,128]{2,1,0:T(8,128)(2,1)} %reshape.273), calls=%async_computation.2 | async-start | bytes 262144 | tf_op jit(solution)/shard_map/all_to_all | solution.py:110
  81.9 6.5 %copy-start.3 = (f32[512]{0:T(512)S(1)}, f32[512]{0:T(512)}, u32[]{:S(2)}) copy-start(f32[512]{0:T(512)} %param.12) | copy-start | bytes 6148
  113.4 8.4 %copy-start.1 = (bf16[6144,512]{1,0:T(8,128)(2,1)S(1)}, bf16[6144,512]{1,0:T(8,128)(2,1)}, u32[]{:S(2)}) copy-start(bf16[6144,512]{1,0:T(8,128)(2,1)} %all-gather.2.cloned.1.call-done) | copy-start | bytes 18874372
  126.1 16.4 %all-to-all-start.4 = ((bf16[4,272,384]{2,1,0:T(8,128)(2,1)}), bf16[4,272,384]{2,1,0:T(8,128)(2,1)S(1)}, u32[]{:S(2)}, u32[]{:S(2)}) async-start(bf16[4,272,384]{2,1,0:T(8,128)(2,1)} %pad_maximum_fusion), calls=%async_computation.4 | async-start | bytes 1671168 | tf_op jit(solution)/shard_map/all_to_all | solution.py:138
Sparse Core Ops, SparseCore 0:
  10.7 102.6 all-gather.1
where the time goes:
time: 152 us; the launch traced here: 151 us
  waiting for transfers between devices  44.8 us (29%)
  starting transfers between devices  44 us (29%)
  blocking collectives  20.5 us (13%)
  matrix products  14.7 us (10%)
  between operations  14.5 us (10%)
  local copies, waits for them, and re-layouts  7.42 us (5%)
  other arithmetic  5.33 us (4%)
    all_to_all x1, blocking collectives, per_device(): acts = lax.all_to_all(message, 'y', 0, 0, tiled=True)  20.5 us
    all_to_all x1, starting transfers between devices, per_device(): lax.all_to_all(jnp.concatenate([out, logs], axis=1), INNER, 0, 0, tiled=T...  20.1 us
    all_to_all x1, waiting for transfers between devices, per_device(): lax.all_to_all(jnp.broadcast_to(total[None], (quads,) + total.shape), 'za...  17.3 us
    all_to_all x1, starting transfers between devices, per_device(): lax.all_to_all(jnp.broadcast_to(total[None], (quads,) + total.shape), 'za...  13.7 us
    all_to_all x1, waiting for transfers between devices, per_device(): shares = lax.all_to_all(with_rows(partial, squares), 'x', 0, 0, tiled=True)  11.7 us
    dot_general x16, matrix products, per_device(): lax.dot_general(acts[i, :tokens], gathered[j, i], (((1,), (1,)), ((), ())...  11.6 us
    all_to_all x1, waiting for transfers between devices, per_device(): lax.all_to_all(jnp.concatenate([out, logs], axis=1), INNER, 0, 0, tiled=T...  5.96 us
    all_to_all x1, waiting for transfers between devices, per_device(): back = lax.all_to_all(states, INNER, 0, 0, tiled=True)  5.68 us
  transfers between devices with their start and end apart: 6, of which 5 were waited for; matrix products, arithmetic and copies ran while one was open for 8% of the time, Pallas kernels for 0%

commit v1 on v0

--- a/solution.py
+++ b/solution.py
@@ -61,7 +61,16 @@
     nx, ny = (lax.axis_size("x"), lax.axis_size("y"))
     swap = [(a * ny + b, b * ny + a) for a in range(ny) for b in range(ny)]
     moved = lax.ppermute(out_weight.T, ("zb", "y"), swap)
-    gathered = lax.all_gather(moved, CTX, axis=0, tiled=True)
+    _trace_spots = lambda sample: jnp.concatenate(
+        lax.all_to_all(
+            jnp.stack([sample for _ in range(lax.axis_size(CTX))], 0),
+            CTX,
+            concat_axis=0,
+            split_axis=0,
+        ),
+        0,
+    )
+    gathered = _trace_spots(moved)
     cols = out_weight.shape[1] * parts // (nx * ny)
     gathered = gathered.reshape(nx, ny, cols, out_weight.shape[0])
     q = queries.reshape(tokens, heads, DH)

time: 152 us -> 420 us (2.76); the launches traced: 151 us -> 414 us
  waiting for transfers between devices: 44.8 us -> 328 us
  blocking collectives: 20.5 us -> 0 us
  between operations: 14.5 us -> 1.13 us
  matrix products: 14.7 us -> 24.1 us
    all_to_all x0 -> x2, waiting for transfers between devices: none -> 294 us  [the longest x1 274 us: per_device(): lax.all_to_all(jnp.stack([sample for _ in range(lax.axis_size(CTX))], 0),...]
    all_to_all x1 -> x0, blocking collectives: 20.5 us -> none  [per_device(): acts = lax.all_to_all(message, 'y', 0, 0, tiled=True)]
    all_to_all x0 -> x2, starting transfers between devices: none -> 12.6 us  [the longest x1 8.46 us: per_device(): lax.all_to_all(jnp.stack([sample for _ in range(lax.axis_size(CTX))], 0),...]
    all_to_all x1, starting transfers between devices: 20.1 us -> 10.1 us  [per_device(): lax.all_to_all(jnp.concatenate([out, logs], axis=1), INNER, 0, 0, tiled=T...]
    dot_general x16, matrix products: 11.6 us -> 21 us  [per_device(): lax.dot_general(acts[i, :tokens], gathered[j, i], (((1,), (1,)), ((), ())...]
    all_to_all x1, waiting for transfers between devices: 17.3 us -> 11.9 us  [per_device(): lax.all_to_all(jnp.broadcast_to(total[None], (quads,) + total.shape), 'za...]
    all_to_all x1, starting transfers between devices: 13.7 us -> 9.46 us  [per_device(): lax.all_to_all(jnp.broadcast_to(total[None], (quads,) + total.shape), 'za...]
  transfers between devices with their start and end apart: 6 -> 7, of which waited for: 5 -> 6; matrix products, arithmetic and copies ran while one was open for 8% -> 1% of each run, Pallas kernels for 0% -> 0%
where the time goes in v1:
time: 420 us; the launch traced here: 414 us
  waiting for transfers between devices  328 us (78%)
  starting transfers between devices  43.9 us (10%)
  matrix products  24.1 us (6%)
  local copies, waits for them, and re-layouts  11.1 us (3%)
  other arithmetic  5.33 us (1%)
    all_to_all x1, waiting for transfers between devices, per_device(): lax.all_to_all(jnp.stack([sample for _ in range(lax.axis_size(CTX))], 0),...  274 us
    dot_general x16, matrix products, per_device(): lax.dot_general(acts[i, :tokens], gathered[j, i], (((1,), (1,)), ((), ())...  21 us
    all_to_all x1, waiting for transfers between devices, per_device(): acts = lax.all_to_all(message, 'y', 0, 0, tiled=True)  19.1 us
    all_to_all x1, waiting for transfers between devices, per_device(): lax.all_to_all(jnp.broadcast_to(total[None], (quads,) + total.shape), 'za...  11.9 us
    all_to_all x1, waiting for transfers between devices, per_device(): shares = lax.all_to_all(with_rows(partial, squares), 'x', 0, 0, tiled=True)  11.5 us
    all_to_all x1, starting transfers between devices, per_device(): lax.all_to_all(jnp.concatenate([out, logs], axis=1), INNER, 0, 0, tiled=T...  10.1 us
    all_to_all x1, starting transfers between devices, per_device(): lax.all_to_all(jnp.broadcast_to(total[None], (quads,) + total.shape), 'za...  9.46 us
    all_to_all x1, starting transfers between devices, per_device(): lax.all_to_all(jnp.stack([sample for _ in range(lax.axis_size(CTX))], 0),...  8.46 us
  transfers between devices with their start and end apart: 7, of which 6 were waited for; matrix products, arithmetic and copies ran while one was open for 1% of the time, Pallas kernels for 0%

profile of v1, /device:TPU:1, one launch (start us, length us, event | category | flops | bytes accessed | tf_op | source)
XLA Modules:
  0.0 413.7 jit_solution(12913365220770992574)
XLA Ops:
  1.4 1.2 reduce-window.6
  3.2 1.1 copy.88
  4.3 1.2 convolution_convert_fusion
  6.3 10.1 %all-to-all-start = ((bf16[8,72,128]{2,1,0:T(8,128)(2,1)}), bf16[8,72,128]{2,1,0:T(8,128)(2,1)S(1)}, u32[]{:S(2)}, u32[]{:S(2)}) async-start(bf16[8,72,128]{2,1,0:T(8,128)(2,1)} %pad_maximum_fusion.2), calls=%async_computation | async-start | bytes 294912 | tf_op jit(solution)/shard_map/all_to_all | solution.py:88
  16.4 6.0 %all-to-all-done = bf16[8,72,128]{2,1,0:T(8,128)(2,1)S(1)} async-done(((bf16[8,72,128]{2,1,0:T(8,128)(2,1)}), bf16[8,72,128]{2,1,0:T(8,128)(2,1)S(1)}, u32[]{:S(2)}, u32[]{:S(2)}) %all-to-all-start) | async-done | bytes 147488 | tf_op jit(solution)/shard_map/all_to_all | solution.py:88
  24.2 9.5 %all-to-all-start.1 = ((f32[4,72,128]{2,1,0:T(8,128)}), f32[4,72,128]{2,1,0:T(8,128)S(1)}, u32[]{:S(2)}, u32[]{:S(2)}) async-start(f32[4,72,128]{2,1,0:T(8,128)} %broadcast_in_dim.38), calls=%async_computation.1 | async-start | bytes 294912 | tf_op jit(solution)/shard_map/all_to_all | solution.py:101
  34.6 11.9 %all-to-all-done.1 = f32[4,72,128]{2,1,0:T(8,128)S(1)} async-done(((f32[4,72,128]{2,1,0:T(8,128)}), f32[4,72,128]{2,1,0:T(8,128)S(1)}, u32[]{:S(2)}, u32[]{:S(2)}) %all-to-all-start.1) | async-done | bytes 147488 | tf_op jit(solution)/shard_map/all_to_all | solution.py:101
  48.4 7.0 %all-to-all-start.2 = ((bf16[8,64,128]{2,1,0:T(8,128)(2,1)}), bf16[8,64,128]{2,1,0:T(8,128)(2,1)S(1)}, u32[]{:S(2)}, u32[]{:S(2)}) async-start(bf16[8,64,128]{2,1,0:T(8,128)(2,1)} %reshape.272), calls=%async_computation.2 | async-start | bytes 262144 | tf_op jit(solution)/shard_map/all_to_all | solution.py:119
  56.1 5.1 %all-to-all-done.2 = bf16[8,64,128]{2,1,0:T(8,128)(2,1)S(1)} async-done(((bf16[8,64,128]{2,1,0:T(8,128)(2,1)}), bf16[8,64,128]{2,1,0:T(8,128)(2,1)S(1)}, u32[]{:S(2)}, u32[]{:S(2)}) %all-to-all-start.2) | async-done | bytes 131104 | tf_op jit(solution)/shard_map/all_to_all | solution.py:119
  63.2 4.2 %all-to-all-start.3 = ((bf16[4,272,512]{2,1,0:T(8,128)(2,1)}), bf16[4,272,512]{2,1,0:T(8,128)(2,1)S(1)}, u32[]{:S(2)}, u32[]{:S(2)}) async-start(bf16[4,272,512]{2,1,0:T(8,128)(2,1)} %broadcast_in_dim.40), calls=%async_computation.3 | async-start | bytes 2228224 | tf_op jit(solution)/shard_map/all_to_all | solution.py:129
  68.1 19.1 %all-to-all-done.3 = bf16[4,272,512]{2,1,0:T(8,128)(2,1)S(1)} async-done(((bf16[4,272,512]{2,1,0:T(8,128)(2,1)}), bf16[4,272,512]{2,1,0:T(8,128)(2,1)S(1)}, u32[]{:S(2)}, u32[]{:S(2)}) %all-to-all-start.3) | async-done | bytes 1114144 | tf_op jit(solution)/shard_map/all_to_all | solution.py:129
  87.1 3.4 stack.20
  90.5 8.5 %all-to-all-start.4 = ((bf16[32,192,512]{2,1,0:T(8,128)(2,1)}), bf16[32,192,512]{2,1,0:T(8,128)(2,1)}, u32[]{:S(2)}, u32[]{:S(2)}) async-start(bf16[32,192,512]{2,1,0:T(8,128)(2,1)} %stack.20), calls=%async_computation.4 | async-start | bytes 12582912 | tf_op jit(solution)/shard_map/all_to_all | solution.py:65
  99.2 274.5 %all-to-all-done.4 = bf16[32,192,512]{2,1,0:T(8,128)(2,1)} async-done(((bf16[32,192,512]{2,1,0:T(8,128)(2,1)}), bf16[32,192,512]{2,1,0:T(8,128)(2,1)}, u32[]{:S(2)}, u32[]{:S(2)}) %all-to-all-start.4) | async-done | bytes 6291488 | tf_op jit(solution)/shard_map/all_to_all | solution.py:65
  373.7 1.3 fusion.23
  375.0 1.3 fusion.22
  376.3 1.3 fusion.21
  377.6 1.3 fusion.20
  378.9 1.3 convolution_add_fusion.11
  380.2 1.3 convolution_add_fusion.10
  381.6 1.3 fusion.11
  382.9 1.3 convolution_add_fusion.8
  384.2 1.3 convolution_add_fusion.7
  385.5 1.3 fusion.10
  386.9 1.3 convolution_add_fusion.5
  388.2 1.3 convolution_add_fusion.4
  389.5 1.3 fusion.9
  390.8 1.3 convolution_add_fusion.2
  392.1 1.3 convolution_add_fusion.1
  393.5 1.3 fusion.8
  395.8 4.0 all-to-all-start.5
  400.4 11.5 %all-to-all-done.5 = bf16[4,272,384]{2,1,0:T(8,128)(2,1)S(1)} async-done(((bf16[4,272,384]{2,1,0:T(8,128)(2,1)}), bf16[4,272,384]{2,1,0:T(8,128)(2,1)S(1)}, u32[]{:S(2)}, u32[]{:S(2)}) %all-to-all-start.5) | async-done | bytes 835616 | tf_op jit(solution)/shard_map/all_to_all | solution.py:147
  (94 shorter events, 13.4 us)
Async XLA Ops:
  0.6 54.8 %copy-start = (bf16[256,512]{1,0:T(8,128)(2,1)S(1)}, bf16[256,512]{1,0:T(8,128)(2,1)}, u32[]{:S(2)}) copy-start(bf16[256,512]{1,0:T(8,128)(2,1)} %param.7) | copy-start | bytes 786436
  6.3 16.1 %all-to-all-start = ((bf16[8,72,128]{2,1,0:T(8,128)(2,1)}), bf16[8,72,128]{2,1,0:T(8,128)(2,1)S(1)}, u32[]{:S(2)}, u32[]{:S(2)}) async-start(bf16[8,72,128]{2,1,0:T(8,128)(2,1)} %pad_maximum_fusion.2), calls=%async_computation | async-start | bytes 294912 | tf_op jit(solution)/shard_map/all_to_all | solution.py:88
  23.5 32.0 %copy-start.2 = (bf16[256,512]{1,0:T(8,128)(2,1)S(1)}, bf16[256,512]{1,0:T(8,128)(2,1)}, u32[]{:S(2)}) copy-start(bf16[256,512]{1,0:T(8,128)(2,1)} %param.9) | copy-start | bytes 786436
  24.2 22.2 %all-to-all-start.1 = ((f32[4,72,128]{2,1,0:T(8,128)}), f32[4,72,128]{2,1,0:T(8,128)S(1)}, u32[]{:S(2)}, u32[]{:S(2)}) async-start(f32[4,72,128]{2,1,0:T(8,128)} %broadcast_in_dim.38), calls=%async_computation.1 | async-start | bytes 294912 | tf_op jit(solution)/shard_map/all_to_all | solution.py:101
  48.4 12.9 %all-to-all-start.2 = ((bf16[8,64,128]{2,1,0:T(8,128)(2,1)}), bf16[8,64,128]{2,1,0:T(8,128)(2,1)S(1)}, u32[]{:S(2)}, u32[]{:S(2)}) async-start(bf16[8,64,128]{2,1,0:T(8,128)(2,1)} %reshape.272), calls=%async_computation.2 | async-start | bytes 262144 | tf_op jit(solution)/shard_map/all_to_all | solution.py:119
  56.1 5.9 %copy-start.1 = (f32[512]{0:T(512)S(1)}, f32[512]{0:T(512)}, u32[]{:S(2)}) copy-start(f32[512]{0:T(512)} %param.12) | copy-start | bytes 6148
  62.1 5.3 %copy-start.3 = (bf16[512,192]{0,1:T(8,128)(2,1)S(1)}, bf16[512,192]{0,1:T(8,128)(2,1)}, u32[]{:S(2)}) copy-start(bf16[512,192]{0,1:T(8,128)(2,1)} %param.13) | copy-start | bytes 589828
  63.2 23.9 %all-to-all-start.3 = ((bf16[4,272,512]{2,1,0:T(8,128)(2,1)}), bf16[4,272,512]{2,1,0:T(8,128)(2,1)S(1)}, u32[]{:S(2)}, u32[]{:S(2)}) async-start(bf16[4,272,512]{2,1,0:T(8,128)(2,1)} %broadcast_in_dim.40), calls=%async_computation.3 | async-start | bytes 2228224 | tf_op jit(solution)/shard_map/all_to_all | solution.py:129
  67.4 0.7 collective-permute-start
  90.5 283.2 %all-to-all-start.4 = ((bf16[32,192,512]{2,1,0:T(8,128)(2,1)}), bf16[32,192,512]{2,1,0:T(8,128)(2,1)}, u32[]{:S(2)}, u32[]{:S(2)}) async-start(bf16[32,192,512]{2,1,0:T(8,128)(2,1)} %stack.20), calls=%async_computation.4 | async-start | bytes 12582912 | tf_op jit(solution)/shard_map/all_to_all | solution.py:65
  395.8 16.2 %all-to-all-start.5 = ((bf16[4,272,384]{2,1,0:T(8,128)(2,1)}), bf16[4,272,384]{2,1,0:T(8,128)(2,1)S(1)}, u32[]{:S(2)}, u32[]{:S(2)}) async-start(bf16[4,272,384]{2,1,0:T(8,128)(2,1)} %pad_maximum_fusion), calls=%async_computation.5 | async-start | bytes 1671168 | tf_op jit(solution)/shard_map/all_to_all | solution.py:147
